TPU v7x, 32 devices: a whole 2x2x4 slice. The times are simulated.
32 devices in a mesh: groups: 1, expert: 16 (over z, y, core), tensor: 2 (over x).
Axes of the slice: x: 2, y: 2, z: 4, core: 2. Of those that a mesh axis runs over, the one named last changes fastest.
Arguments:
- tokens: bfloat16 [2048, 4096], P(('groups', 'expert')), may hold values from -6 to 6
- expert_ids: int32 [2048, 8], P(('groups', 'expert')), may hold values from 0 to 15, all different within a row; in each aligned block of 128 rows (0 to 127, 128 to 255, ...) at most 96 rows name the same one
- route_weights: float32 [2048, 8], P(('groups', 'expert')), may hold values from 0.1 to 1
- gate_w: bfloat16 [16, 4096, 1536], P('expert', None, 'tensor'), may hold values from -0.09375 to 0.09375
- up_w: bfloat16 [16, 4096, 1536], P('expert', None, 'tensor'), may hold values from -0.09375 to 0.09375
- down_w: bfloat16 [16, 1536, 4096], P('expert', 'tensor'), may hold values from -0.15625 to 0.15625
Outputs:
- moe_out: bfloat16 [2048, 4096], P(('groups', 'expert'), 'tensor')
Inputs may be any that keep to these rules, and one draw needn't show every extreme that they name: `expert_ids`: each row names 8 different experts. Among the rows of one device (aligned blocks of 128 rows) no expert is named more than 96 times, a bound that some block reaches.
All inputs are finite; a program needn't handle non-finite values.
Results may differ from a plain program's by a relative error of at most 0.014.
Values may be sent and summed in bfloat16 or wider, within the bound.
A program may use at most 128 MiB of HBM per device.

v0:
```python
import jax
import jax.numpy as jnp
from jax import lax
from jax.sharding import PartitionSpec as P


def shards(tokens, expert_ids, route_weights, gate_w, up_w, down_w):
    tok_rows, width = tokens.shape
    top_count = expert_ids.shape[1]
    local_experts = gate_w.shape[0]
    expert_devices = lax.axis_size("expert")
    experts_all = local_experts * expert_devices
    capacity = min(tok_rows, 3 * tok_rows * top_count // (2 * experts_all))
    flat_ids = expert_ids.reshape(-1)
    onehot = (flat_ids[:, None] == jnp.arange(experts_all, dtype=jnp.int32)[None, :]).astype(
        jnp.int32
    )
    before = jnp.cumsum(onehot, axis=0) - onehot
    slot = jnp.sum(before * onehot, axis=1)
    destination = flat_ids * capacity + slot
    token_index = jnp.arange(tok_rows * top_count, dtype=jnp.int32) // top_count
    source = jnp.zeros((experts_all * capacity,), jnp.int32).at[destination].set(token_index)
    filled = jnp.zeros((experts_all * capacity,), jnp.bool_).at[destination].set(True)
    outgoing = jnp.where(filled[:, None], tokens[source], jnp.zeros((), tokens.dtype))
    outgoing = outgoing.reshape(experts_all, capacity, tokens.shape[1])
    received = lax.all_to_all(outgoing, "expert", split_axis=0, concat_axis=0, tiled=True)
    slots_in = received.shape[1]
    rows = received.reshape(expert_devices, local_experts, slots_in, width)
    rows = rows.transpose(1, 0, 2, 3).reshape(local_experts, expert_devices * slots_in, width)
    gate = jnp.einsum("erd,edf->erf", rows, gate_w, preferred_element_type=jnp.float32)
    up_part = jnp.einsum("erd,edf->erf", rows, up_w, preferred_element_type=jnp.float32)
    hidden = (jax.nn.silu(gate) * up_part).astype(jnp.bfloat16)
    partial_value = jnp.einsum("erf,efd->erd", hidden, down_w, preferred_element_type=jnp.float32)
    summed = lax.psum_scatter(
        partial_value.astype(jnp.bfloat16), "tensor", scatter_dimension=2, tiled=True
    )
    share = summed.shape[2]
    going_back = summed.reshape(local_experts, expert_devices, slots_in, share)
    going_back = going_back.transpose(1, 0, 2, 3).reshape(experts_all, slots_in, share)
    returned = lax.all_to_all(going_back, "expert", split_axis=0, concat_axis=0, tiled=True)
    share_cols = returned.shape[2]
    flat_back = returned.reshape(experts_all * capacity, share_cols)
    picked = flat_back[destination].reshape(tok_rows, top_count, share_cols)
    mixed = jnp.einsum("tk,tkd->td", route_weights, picked.astype(jnp.float32))
    return mixed.astype(jnp.bfloat16)


def solution(mesh):
    in_specs = (
        P(("groups", "expert"), None),
        P(("groups", "expert"), None),
        P(("groups", "expert"), None),
        P("expert", None, "tensor"),
        P("expert", None, "tensor"),
        P("expert", "tensor", None),
    )
    out_specs = P(("groups", "expert"), "tensor")
    return jax.shard_map(shards, mesh=mesh, in_specs=in_specs, out_specs=out_specs, check_vma=False)
```

profile of v0, /device:TPU:13, one launch (start us, length us, event | category | flops | bytes accessed | tf_op | source)
XLA Modules:
  0.0 667.2 jit_solution(3514439401842417183)
XLA Ops:
  6.5 0.0 copy-start
  6.5 0.0 reduce-scatter.2.cloned.1.call-start
  6.5 0.9 copy.10
  7.4 0.1 eq.29
  7.5 0.1 eq.25
  7.6 0.7 broadcast_multiply_fusion
  8.3 4.5 reduce-window.6
  12.8 0.1 slice.12
  12.9 0.1 copy.12
  13.1 0.1 copy.13
  13.1 0.1 broadcast_add_fusion
  13.2 0.1 copy.9
  13.3 0.1 mul.30
  13.5 4.3 scatter_custom_fusion.1
  17.9 4.3 scatter_custom_fusion
  22.2 0.1 broadcast_in_dim.30
  22.3 0.0 copy-done
  22.3 9.5 %gather_fusion = bf16[1536,4096]{1,0:T(8,128)(2,1)} fusion(bf16[128,4096]{1,0:T(8,128)(2,1)S(1)} %copy-done, s32[2048]{0:T(1024)S(1)} %pad_clamp_fusion), kind=kCustom, calls=%fused_computation | custom fusion | bytes 25171968 | tf_op jit(solution)/shard_map/gather | solution.py:24
  31.8 6.4 broadcast_select_fusion
  38.2 0.0 copy-start.3
  38.2 278.6 %all_to_all.10 = bf16[16,96,4096]{2,1,0:T(8,128)(2,1)S(1)} all-to-all(bf16[16,96,4096]{2,1,0:T(8,128)(2,1)S(1)} %broadcast_select_fusion), channel_id=1, replica_groups=mesh['groups'=1,'expert'=16,'tensor'=2] {'expert'}, dimensions={0} | all-to-all | bytes 25165824 | tf_op jit(solution)/shard_map/all_to_all | solution.py:26
  316.8 11.4 %fusion.2 = f32[1536,768]{1,0:T(8,128)} fusion(bf16[1536,4096]{1,0:T(8,128)(2,1)S(1)} %bitcast.49, bf16[1,4096,768]{2,1,0:T(8,128)(2,1)S(1)} %copy-done.3), kind=kOutput, calls=%fused_computation.8 | convolution fusion | flops 9663676416 | bytes 23592960 | tf_op jit(solution)/shard_map/erd,edf->erf/dot_general | solution.py:31
  328.2 13.5 %multiply_convert_fusion = bf16[1536,768]{1,0:T(8,128)(2,1)S(1)} fusion(f32[1536,768]{1,0:T(8,128)} %fusion.2, bf16[1536,4096]{1,0:T(8,128)(2,1)S(1)} %bitcast.50, bf16[1,4096,768]{2,1,0:T(8,128)(2,1)} %param.9), kind=kOutput, calls=%fused_computation.12 | convolution fusion | flops 9670754304 | bytes 25952256 | tf_op jit(solution)/shard_map/erd,edf->erf/dot_general | solution.py:30
  341.7 12.4 %fusion = bf16[1,1536,4096]{2,1,0:T(8,128)(2,1)} fusion(bf16[1536,768]{1,0:T(8,128)(2,1)S(1)} %multiply_convert_fusion, bf16[1,768,4096]{2,1,0:T(8,128)(2,1)S(1)} %bitcast.60), kind=kOutput, calls=%fused_computation.5 | convolution fusion | flops 9669967872 | bytes 21233664 | tf_op jit(solution)/shard_map/erf,efd->erd/dot_general | solution.py:33
  354.1 0.0 reduce-scatter.2.cloned.1.call-update
  354.1 145.2 %reduce-scatter.2.cloned.1.call-done = bf16[1,1536,2048]{2,1,0:T(8,128)(2,1)} async-done(((bf16[1,1536,4096]{2,1,0:T(8,128)(2,1)}), bf16[1,1536,2048]{2,1,0:T(8,128)(2,1)}) %reduce-scatter.2.cloned.1.call-update) | async-done | bytes 6291472 | tf_op jit(solution)/shard_map/reduce_scatter | solution.py:34
  499.3 6.7 all-to-all-start.1
  506.0 0.1 copy.14
  506.1 137.2 %all-to-all-done.1 = bf16[16,96,2048]{2,1,0:T(8,128)(2,1)} async-done(((bf16[16,96,2048]{2,1,0:T(8,128)(2,1)}), bf16[16,96,2048]{2,1,0:T(8,128)(2,1)}, u32[]{:S(2)}, u32[]{:S(2)}) %all-to-all-start.1) | async-done | bytes 6291488 | tf_op jit(solution)/shard_map/all_to_all | solution.py:40
  643.4 12.5 %gather_fusion.1 = bf16[1024,2048]{1,0:T(8,128)(2,1)} fusion(bf16[1536,2048]{1,0:T(8,128)(2,1)} %bitcast.11, s32[1024]{0:T(1024)S(1)} %broadcast_clamp_fusion), kind=kCustom, calls=%fused_computation.1 | custom fusion | bytes 8392704 | tf_op jit(solution)/shard_map/gather | solution.py:43
  655.9 3.4 fusion.8
  659.3 1.1 copy.19
  (20 shorter events, 0.1 us)
Async XLA Ops:
  6.5 15.8 %copy-start = (bf16[128,4096]{1,0:T(8,128)(2,1)S(1)}, bf16[128,4096]{1,0:T(8,128)(2,1)}, u32[]{:S(2)}) copy-start(bf16[128,4096]{1,0:T(8,128)(2,1)} %param.6) | copy-start | bytes 3145732
  6.5 492.8 %reduce-scatter.2.cloned.1.call-start = ((), (), s32[]{:S(2)}) async-start(), calls=%async_computation.3 | async-start | bytes 18874368 | tf_op jit(solution)/shard_map/reduce_scatter | solution.py:34
  38.2 278.6 %copy-start.3 = (bf16[1,4096,768]{2,1,0:T(8,128)(2,1)S(1)}, bf16[1,4096,768]{2,1,0:T(8,128)(2,1)}, u32[]{:S(2)}) copy-start(bf16[1,4096,768]{2,1,0:T(8,128)(2,1)} %param.10) | copy-start | bytes 18874372
  316.8 25.0 %slice-start = ((s8[6291456]{0:T(1024)(128)(4,1)}), s8[2097152]{0:T(1024)(128)(4,1)S(1)}, s32[]{:S(2)}) async-start(s8[6291456]{0:T(1024)(128)(4,1)} %bitcast.59), calls=%async_computation.4 | async-start | bytes 4194304
  328.2 13.5 %slice-start.1 = ((s8[6291456]{0:T(1024)(128)(4,1)}), s8[4194304]{0:T(1024)(128)(4,1)S(1)}, s32[]{:S(2)}) async-start(s8[6291456]{0:T(1024)(128)(4,1)} %bitcast.59), calls=%async_computation.5 | async-start | bytes 8388608
  499.3 6.7 copy-start.2
  499.3 144.1 %all-to-all-start.1 = ((bf16[16,96,2048]{2,1,0:T(8,128)(2,1)}), bf16[16,96,2048]{2,1,0:T(8,128)(2,1)}, u32[]{:S(2)}, u32[]{:S(2)}) async-start(bf16[16,96,2048]{2,1,0:T(8,128)(2,1)} %bitcast.51), calls=%async_computation.2 | async-start | bytes 12582912 | tf_op jit(solution)/shard_map/all_to_all | solution.py:40
  643.4 17.0 %copy-start.1 = (bf16[128,4096]{1,0:T(8,128)(2,1)S(1)}, bf16[128,4096]{1,0:T(8,128)(2,1)}, u32[]{:S(2)}) copy-start(bf16[128,4096]{1,0:T(8,128)(2,1)} %param.6) | copy-start | bytes 3145732
Sparse Core Ops, SparseCore 0:
  354.3 145.0 reduce-scatter.1
where the time goes:
time: 668 us; the launch traced here: 667 us
  waiting for transfers between devices  282 us (42%)
  blocking collectives  279 us (42%)
  matrix products  40.7 us (6%)
  local copies, waits for them, and re-layouts  33.6 us (5%)
  between operations  13.5 us (2%)
  other arithmetic  11.7 us (2%)
    all_to_all x1, blocking collectives, shards(): lax.all_to_all(outgoing, 'expert', split_axis=0, concat_axis=0, tiled=True)  279 us
    reduce_scatter x1, waiting for transfers between devices, shards(): lax.psum_scatter(partial_value.astype(jnp.bfloat16), 'tensor', scatter_di...  145 us
    all_to_all x1, waiting for transfers between devices, shards(): lax.all_to_all(going_back, 'expert', split_axis=0, concat_axis=0, tiled=T...  137 us
    dot_general x1, matrix products, shards(): jnp.einsum('erd,edf->erf', rows, gate_w, preferred_element_type=jnp.float32)  13.5 us
  transfers between devices with their start and end apart: 2, of which 2 were waited for; matrix products, arithmetic and copies ran while one was open for 0% of the time, Pallas kernels for 0%

commit v1 on v0

--- a/solution.py
+++ b/solution.py
@@ -2,6 +2,29 @@
 import jax.numpy as jnp
 from jax import lax
 from jax.sharding import PartitionSpec as P
+
+
+def in_blocks(x, dim, length):
+    lengths = x.shape
+    blocks = x.reshape(*lengths[:dim], length, lengths[dim] // length, *lengths[dim + 1 :])
+    return jnp.moveaxis(blocks, dim, 0)
+
+
+def joined_along(blocks, dim):
+    shape = list(blocks.shape[1:])
+    shape[dim] *= blocks.shape[0]
+    return jnp.moveaxis(blocks, 0, dim).reshape(shape)
+
+
+def swapped_with_each(x, axis, split_dim, concat_dim):
+    count, index = (lax.axis_size(axis), lax.axis_index(axis))
+    blocks = in_blocks(x, split_dim, count)
+    done = [blocks[index]]
+    for hop in range(1, count):
+        sent = blocks[index ^ hop]
+        done.append(lax.ppermute(sent, axis, [(i, i ^ hop) for i in range(count)]))
+    blocks = jnp.stack(done)[index ^ jnp.arange(count)]
+    return joined_along(blocks, concat_dim)
 
 
 def shards(tokens, expert_ids, route_weights, gate_w, up_w, down_w):
@@ -37,7 +60,7 @@
     share = summed.shape[2]
     going_back = summed.reshape(local_experts, expert_devices, slots_in, share)
     going_back = going_back.transpose(1, 0, 2, 3).reshape(experts_all, slots_in, share)
-    returned = lax.all_to_all(going_back, "expert", split_axis=0, concat_axis=0, tiled=True)
+    returned = swapped_with_each(going_back, "expert", 0, 0)
     share_cols = returned.shape[2]
     flat_back = returned.reshape(experts_all * capacity, share_cols)
     picked = flat_back[destination].reshape(tok_rows, top_count, share_cols)

time: 668 us -> 695 us (1.040)
  local copies, waits for them, and re-layouts: 33.6 us -> 56.6 us
  starting transfers between devices: 6.66 us -> 18.4 us
  waiting for transfers between devices: 282 us -> 273 us
    all_to_all x1 -> x0, waiting for transfers between devices: 137 us -> none  [shards(): lax.all_to_all(going_back, 'expert', split_axis=0, concat_axis=0, tiled=T...]
    ppermute x0 -> x15, waiting for transfers between devices: none -> 128 us  [swapped_with_each(): done.append(lax.ppermute(sent, axis, [(i, i ^ hop) for i in range(count)]))]
    ppermute x0 -> x15, starting transfers between devices: none -> 18.4 us  [swapped_with_each(): done.append(lax.ppermute(sent, axis, [(i, i ^ hop) for i in range(count)]))]
    unnamed x14 -> x28, local copies, waits for them, and re-layouts: 1.04 us -> 12.5 us
  transfers between devices with their start and end apart: 2 -> 16, of which waited for: 2 -> 12; matrix products, arithmetic and copies ran while one was open for 0% -> 2% of each run, Pallas kernels for 0% -> 0%
where the time goes in v1:
time: 695 us; the launch traced here: 693 us
  blocking collectives  279 us (40%)
  waiting for transfers between devices  273 us (39%)
  local copies, waits for them, and re-layouts  56.6 us (8%)
  matrix products  40.8 us (6%)
  starting transfers between devices  18.4 us (3%)
  between operations  13.7 us (2%)
  other arithmetic  11.8 us (2%)
    all_to_all x1, blocking collectives, shards(): lax.all_to_all(outgoing, 'expert', split_axis=0, concat_axis=0, tiled=True)  279 us
    reduce_scatter x1, waiting for transfers between devices, shards(): lax.psum_scatter(partial_value.astype(jnp.bfloat16), 'tensor', scatter_di...  144 us
    ppermute x15, waiting for transfers between devices, swapped_with_each(): done.append(lax.ppermute(sent, axis, [(i, i ^ hop) for i in range(count)]))  128 us
    ppermute x15, starting transfers between devices, swapped_with_each(): done.append(lax.ppermute(sent, axis, [(i, i ^ hop) for i in range(count)]))  18.4 us
  transfers between devices with their start and end apart: 16, of which 12 were waited for; matrix products, arithmetic and copies ran while one was open for 2% of the time, Pallas kernels for 0%

profile of v1, /device:TPU:13, one launch (start us, length us, event | category | flops | bytes accessed | tf_op | source)
XLA Modules:
  0.0 692.6 jit_solution(7763921871035388048)
XLA Ops:
  8.3 4.5 reduce-window.6
  13.5 4.3 scatter_custom_fusion.1
  17.9 4.3 scatter_custom_fusion
  22.3 9.5 %gather_fusion = bf16[1536,4096]{1,0:T(8,128)(2,1)} fusion(bf16[128,4096]{1,0:T(8,128)(2,1)S(1)} %copy-done, s32[2048]{0:T(1024)S(1)} %pad_clamp_fusion), kind=kCustom, calls=%fused_computation | custom fusion | bytes 25171968 | tf_op jit(solution)/shard_map/gather | solution.py:47
  31.8 6.4 broadcast_select_fusion
  38.2 278.6 %all_to_all.5 = bf16[16,96,4096]{2,1,0:T(8,128)(2,1)S(1)} all-to-all(bf16[16,96,4096]{2,1,0:T(8,128)(2,1)S(1)} %broadcast_select_fusion), channel_id=1, replica_groups=mesh['groups'=1,'expert'=16,'tensor'=2] {'expert'}, dimensions={0} | all-to-all | bytes 25165824 | tf_op jit(solution)/shard_map/all_to_all | solution.py:49
  316.8 11.4 %fusion.2 = f32[1536,768]{1,0:T(8,128)} fusion(bf16[1536,4096]{1,0:T(8,128)(2,1)S(1)} %bitcast.113, bf16[1,4096,768]{2,1,0:T(8,128)(2,1)S(1)} %copy-done.3), kind=kOutput, calls=%fused_computation.9 | convolution fusion | flops 9663676416 | bytes 23592960 | tf_op jit(solution)/shard_map/erd,edf->erf/dot_general | solution.py:54
  328.2 13.5 %multiply_convert_fusion = bf16[1536,768]{1,0:T(8,128)(2,1)S(1)} fusion(f32[1536,768]{1,0:T(8,128)} %fusion.2, bf16[1536,4096]{1,0:T(8,128)(2,1)S(1)} %bitcast.114, bf16[1,4096,768]{2,1,0:T(8,128)(2,1)} %param.9), kind=kOutput, calls=%fused_computation.13 | convolution fusion | flops 9670754304 | bytes 25952256 | tf_op jit(solution)/shard_map/erd,edf->erf/dot_general | solution.py:53
  341.8 12.5 %fusion = bf16[1,1536,4096]{2,1,0:T(8,128)(2,1)} fusion(bf16[1536,768]{1,0:T(8,128)(2,1)S(1)} %multiply_convert_fusion, bf16[1,768,4096]{2,1,0:T(8,128)(2,1)S(1)} %bitcast.124), kind=kOutput, calls=%fused_computation.6 | convolution fusion | flops 9669967872 | bytes 21233664 | tf_op jit(solution)/shard_map/erf,efd->erd/dot_general | solution.py:56
  355.2 144.3 %reduce-scatter.2.cloned.1.call-done = bf16[1,1536,2048]{2,1,0:T(8,128)(2,1)} async-done(((bf16[1,1536,4096]{2,1,0:T(8,128)(2,1)}), bf16[1,1536,2048]{2,1,0:T(8,128)(2,1)}) %reduce-scatter.2.cloned.1.call-update) | async-done | bytes 6291472 | tf_op jit(solution)/shard_map/reduce_scatter | solution.py:57
  499.5 4.4 dynamic-slice_bitcast_fusion
  505.0 1.4 collective-permute-start.2
  506.7 1.6 collective-permute-start.4
  509.3 6.1 collective-permute-done.1
  515.4 1.5 collective-permute-start.6
  517.7 6.6 collective-permute-done.2
  524.3 2.1 collective-permute-start.7
  528.4 2.1 collective-permute-start.9
  531.2 17.3 %collective-permute-done.5 = bf16[1,96,2048]{2,1,0:T(8,128)(2,1)S(1)} collective-permute-done((bf16[1,96,2048]{2,1,0:T(8,128)(2,1)S(1)}, bf16[1,96,2048]{2,1,0:T(8,128)(2,1)S(1)}, u32[]{:S(2)}, u32[]{:S(2)}) %collective-permute-start.5) | collective-permute-done | bytes 393248 | tf_op jit(solution)/shard_map/ppermute | solution.py:25
  548.6 4.7 collective-permute-start.10
  554.0 3.0 collective-permute-done.6
  558.0 2.5 collective-permute-start.12
  561.3 32.8 %collective-permute-done.8 = bf16[1,96,2048]{2,1,0:T(8,128)(2,1)S(1)} collective-permute-done((bf16[1,96,2048]{2,1,0:T(8,128)(2,1)S(1)}, bf16[1,96,2048]{2,1,0:T(8,128)(2,1)S(1)}, u32[]{:S(2)}, u32[]{:S(2)}) %collective-permute-start.8) | collective-permute-done | bytes 393248 | tf_op jit(solution)/shard_map/ppermute | solution.py:25
  594.8 16.1 %collective-permute-done.9 = bf16[1,96,2048]{2,1,0:T(8,128)(2,1)S(1)} collective-permute-done((bf16[1,96,2048]{2,1,0:T(8,128)(2,1)S(1)}, bf16[1,96,2048]{2,1,0:T(8,128)(2,1)S(1)}, u32[]{:S(2)}, u32[]{:S(2)}) %collective-permute-start.9) | collective-permute-done | bytes 393248 | tf_op jit(solution)/shard_map/ppermute | solution.py:25
  612.0 15.7 %collective-permute-done.10 = bf16[1,96,2048]{2,1,0:T(8,128)(2,1)S(1)} collective-permute-done((bf16[1,96,2048]{2,1,0:T(8,128)(2,1)S(1)}, bf16[1,96,2048]{2,1,0:T(8,128)(2,1)S(1)}, u32[]{:S(2)}, u32[]{:S(2)}) %collective-permute-start.10) | collective-permute-done | bytes 393248 | tf_op jit(solution)/shard_map/ppermute | solution.py:25
  628.5 7.7 %collective-permute-done.11 = bf16[1,96,2048]{2,1,0:T(8,128)(2,1)S(1)} collective-permute-done((bf16[1,96,2048]{2,1,0:T(8,128)(2,1)S(1)}, bf16[1,96,2048]{2,1,0:T(8,128)(2,1)S(1)}, u32[]{:S(2)}, u32[]{:S(2)}) %collective-permute-start.11) | collective-permute-done | bytes 393248 | tf_op jit(solution)/shard_map/ppermute | solution.py:25
  637.0 8.1 %collective-permute-done.12 = bf16[1,96,2048]{2,1,0:T(8,128)(2,1)S(1)} collective-permute-done((bf16[1,96,2048]{2,1,0:T(8,128)(2,1)S(1)}, bf16[1,96,2048]{2,1,0:T(8,128)(2,1)S(1)}, u32[]{:S(2)}, u32[]{:S(2)}) %collective-permute-start.12) | collective-permute-done | bytes 393248 | tf_op jit(solution)/shard_map/ppermute | solution.py:25
  645.9 7.2 %collective-permute-done.13 = bf16[1,96,2048]{2,1,0:T(8,128)(2,1)S(1)} collective-permute-done((bf16[1,96,2048]{2,1,0:T(8,128)(2,1)S(1)}, bf16[1,96,2048]{2,1,0:T(8,128)(2,1)S(1)}, u32[]{:S(2)}, u32[]{:S(2)}) %collective-permute-start.13) | collective-permute-done | bytes 393248 | tf_op jit(solution)/shard_map/ppermute | solution.py:25
  653.9 7.7 %collective-permute-done.14 = bf16[1,96,2048]{2,1,0:T(8,128)(2,1)S(1)} collective-permute-done((bf16[1,96,2048]{2,1,0:T(8,128)(2,1)S(1)}, bf16[1,96,2048]{2,1,0:T(8,128)(2,1)S(1)}, u32[]{:S(2)}, u32[]{:S(2)}) %collective-permute-start.14) | collective-permute-done | bytes 393248 | tf_op jit(solution)/shard_map/ppermute | solution.py:25
  662.4 6.4 gather_fusion.1
  668.7 12.5 %gather_fusion.2 = bf16[1024,2048]{1,0:T(8,128)(2,1)} fusion(bf16[1536,2048]{1,0:T(8,128)(2,1)} %bitcast.111, s32[1024]{0:T(1024)S(1)} %broadcast_clamp_fusion), kind=kCustom, calls=%fused_computation.2 | custom fusion | bytes 8392704 | tf_op jit(solution)/shard_map/gather | solution.py:66
  681.2 3.4 fusion.8
  (67 shorter events, 18.7 us)
Async XLA Ops:
  6.5 15.8 %copy-start = (bf16[128,4096]{1,0:T(8,128)(2,1)S(1)}, bf16[128,4096]{1,0:T(8,128)(2,1)}, u32[]{:S(2)}) copy-start(bf16[128,4096]{1,0:T(8,128)(2,1)} %param.6) | copy-start | bytes 3145732
  6.5 492.9 %reduce-scatter.2.cloned.1.call-start = ((), (), s32[]{:S(2)}) async-start(), calls=%async_computation.2 | async-start | bytes 18874368 | tf_op jit(solution)/shard_map/reduce_scatter | solution.py:57
  38.2 278.6 %copy-start.3 = (bf16[1,4096,768]{2,1,0:T(8,128)(2,1)S(1)}, bf16[1,4096,768]{2,1,0:T(8,128)(2,1)}, u32[]{:S(2)}) copy-start(bf16[1,4096,768]{2,1,0:T(8,128)(2,1)} %param.10) | copy-start | bytes 18874372
  316.8 25.0 %slice-start = ((s8[6291456]{0:T(1024)(128)(4,1)}), s8[2097152]{0:T(1024)(128)(4,1)S(1)}, s32[]{:S(2)}) async-start(s8[6291456]{0:T(1024)(128)(4,1)} %bitcast.123), calls=%async_computation.3 | async-start | bytes 4194304
  328.2 13.5 %slice-start.1 = ((s8[6291456]{0:T(1024)(128)(4,1)}), s8[4194304]{0:T(1024)(128)(4,1)S(1)}, s32[]{:S(2)}) async-start(s8[6291456]{0:T(1024)(128)(4,1)} %bitcast.123), calls=%async_computation.4 | async-start | bytes 8388608
  354.2 0.7 copy-start.2
  503.9 4.4 collective-permute-start
  504.7 10.7 %collective-permute-start.1 = (bf16[1,96,2048]{2,1,0:T(8,128)(2,1)S(1)}, bf16[1,96,2048]{2,1,0:T(8,128)(2,1)S(1)}, u32[]{:S(2)}, u32[]{:S(2)}) collective-permute-start(bf16[1,96,2048]{2,1,0:T(8,128)(2,1)S(1)} %get-tuple-element.18), channel_id=1, source_target_pairs={{0,4},{2,6},{4,0},{6,2},{8,12},{10,14},{12,8},{14,10},{16,20},{18,... | collective-permute-start | bytes 1179656 | tf_op jit(solution)/shard_map/ppermute | solution.py:25
  505.0 19.3 %collective-permute-start.2 = (bf16[1,96,2048]{2,1,0:T(8,128)(2,1)S(1)}, bf16[1,96,2048]{2,1,0:T(8,128)(2,1)S(1)}, u32[]{:S(2)}, u32[]{:S(2)}) collective-permute-start(bf16[1,96,2048]{2,1,0:T(8,128)(2,1)S(1)} %get-tuple-element.17), channel_id=1, source_target_pairs={{0,6},{2,4},{4,2},{6,0},{8,14},{10,12},{12,10},{14,8},{16,22},{18,... | collective-permute-start | bytes 1179656 | tf_op jit(solution)/shard_map/ppermute | solution.py:25
  506.4 20.9 %collective-permute-start.3 = (bf16[1,96,2048]{2,1,0:T(8,128)(2,1)S(1)}, bf16[1,96,2048]{2,1,0:T(8,128)(2,1)S(1)}, u32[]{:S(2)}, u32[]{:S(2)}) collective-permute-start(bf16[1,96,2048]{2,1,0:T(8,128)(2,1)S(1)} %get-tuple-element.16), channel_id=1, source_target_pairs={{0,8},{2,10},{4,12},{6,14},{8,0},{10,2},{12,4},{14,6},{16,24},{18,... | collective-permute-start | bytes 1179656 | tf_op jit(solution)/shard_map/ppermute | solution.py:25
  506.7 21.7 %collective-permute-start.4 = (bf16[1,96,2048]{2,1,0:T(8,128)(2,1)S(1)}, bf16[1,96,2048]{2,1,0:T(8,128)(2,1)S(1)}, u32[]{:S(2)}, u32[]{:S(2)}) collective-permute-start(bf16[1,96,2048]{2,1,0:T(8,128)(2,1)S(1)} %get-tuple-element.15), channel_id=1, source_target_pairs={{0,10},{2,8},{4,14},{6,12},{8,2},{10,0},{12,6},{14,4},{16,26},{18,... | collective-permute-start | bytes 1179656 | tf_op jit(solution)/shard_map/ppermute | solution.py:25
  508.3 40.3 %collective-permute-start.5 = (bf16[1,96,2048]{2,1,0:T(8,128)(2,1)S(1)}, bf16[1,96,2048]{2,1,0:T(8,128)(2,1)S(1)}, u32[]{:S(2)}, u32[]{:S(2)}) collective-permute-start(bf16[1,96,2048]{2,1,0:T(8,128)(2,1)S(1)} %get-tuple-element.14), channel_id=1, source_target_pairs={{0,12},{2,14},{4,8},{6,10},{8,4},{10,6},{12,0},{14,2},{16,28},{18,... | collective-permute-start | bytes 1179656 | tf_op jit(solution)/shard_map/ppermute | solution.py:25
  515.4 41.6 %collective-permute-start.6 = (bf16[1,96,2048]{2,1,0:T(8,128)(2,1)S(1)}, bf16[1,96,2048]{2,1,0:T(8,128)(2,1)S(1)}, u32[]{:S(2)}, u32[]{:S(2)}) collective-permute-start(bf16[1,96,2048]{2,1,0:T(8,128)(2,1)S(1)} %get-tuple-element.13), channel_id=1, source_target_pairs={{0,14},{2,12},{4,10},{6,8},{8,6},{10,4},{12,2},{14,0},{16,30},{18,... | collective-permute-start | bytes 1179656 | tf_op jit(solution)/shard_map/ppermute | solution.py:25
  524.3 33.7 %collective-permute-start.7 = (bf16[1,96,2048]{2,1,0:T(8,128)(2,1)S(1)}, bf16[1,96,2048]{2,1,0:T(8,128)(2,1)S(1)}, u32[]{:S(2)}, u32[]{:S(2)}) collective-permute-start(bf16[1,96,2048]{2,1,0:T(8,128)(2,1)S(1)} %get-tuple-element.12), channel_id=1, source_target_pairs={{0,16},{2,18},{4,20},{6,22},{8,24},{10,26},{12,28},{14,30},{16,0},... | collective-permute-start | bytes 1179656 | tf_op jit(solution)/shard_map/ppermute | solution.py:25
  527.3 66.8 %collective-permute-start.8 = (bf16[1,96,2048]{2,1,0:T(8,128)(2,1)S(1)}, bf16[1,96,2048]{2,1,0:T(8,128)(2,1)S(1)}, u32[]{:S(2)}, u32[]{:S(2)}) collective-permute-start(bf16[1,96,2048]{2,1,0:T(8,128)(2,1)S(1)} %get-tuple-element.11), channel_id=1, source_target_pairs={{0,18},{2,16},{4,22},{6,20},{8,26},{10,24},{12,30},{14,28},{16,2},... | collective-permute-start | bytes 1179656 | tf_op jit(solution)/shard_map/ppermute | solution.py:25
  528.4 82.6 %collective-permute-start.9 = (bf16[1,96,2048]{2,1,0:T(8,128)(2,1)S(1)}, bf16[1,96,2048]{2,1,0:T(8,128)(2,1)S(1)}, u32[]{:S(2)}, u32[]{:S(2)}) collective-permute-start(bf16[1,96,2048]{2,1,0:T(8,128)(2,1)S(1)} %get-tuple-element.10), channel_id=1, source_target_pairs={{0,20},{2,22},{4,16},{6,18},{8,28},{10,30},{12,24},{14,26},{16,4},... | collective-permute-start | bytes 1179656 | tf_op jit(solution)/shard_map/ppermute | solution.py:25
  548.6 79.2 %collective-permute-start.10 = (bf16[1,96,2048]{2,1,0:T(8,128)(2,1)S(1)}, bf16[1,96,2048]{2,1,0:T(8,128)(2,1)S(1)}, u32[]{:S(2)}, u32[]{:S(2)}) collective-permute-start(bf16[1,96,2048]{2,1,0:T(8,128)(2,1)S(1)} %get-tuple-element.9), channel_id=1, source_target_pairs={{0,22},{2,20},{4,18},{6,16},{8,30},{10,28},{12,26},{14,24},{16,6},... | collective-permute-start | bytes 1179656 | tf_op jit(solution)/shard_map/ppermute | solution.py:25
  557.0 79.2 %collective-permute-start.11 = (bf16[1,96,2048]{2,1,0:T(8,128)(2,1)S(1)}, bf16[1,96,2048]{2,1,0:T(8,128)(2,1)S(1)}, u32[]{:S(2)}, u32[]{:S(2)}) collective-permute-start(bf16[1,96,2048]{2,1,0:T(8,128)(2,1)S(1)} %get-tuple-element.8), channel_id=1, source_target_pairs={{0,24},{2,26},{4,28},{6,30},{8,16},{10,18},{12,20},{14,22},{16,8},... | collective-permute-start | bytes 1179656 | tf_op jit(solution)/shard_map/ppermute | solution.py:25
  558.0 87.1 %collective-permute-start.12 = (bf16[1,96,2048]{2,1,0:T(8,128)(2,1)S(1)}, bf16[1,96,2048]{2,1,0:T(8,128)(2,1)S(1)}, u32[]{:S(2)}, u32[]{:S(2)}) collective-permute-start(bf16[1,96,2048]{2,1,0:T(8,128)(2,1)S(1)} %get-tuple-element.7), channel_id=1, source_target_pairs={{0,26},{2,24},{4,30},{6,28},{8,18},{10,16},{12,22},{14,20},{16,10}... | collective-permute-start | bytes 1179656 | tf_op jit(solution)/shard_map/ppermute | solution.py:25
  594.1 59.0 %collective-permute-start.13 = (bf16[1,96,2048]{2,1,0:T(8,128)(2,1)S(1)}, bf16[1,96,2048]{2,1,0:T(8,128)(2,1)S(1)}, u32[]{:S(2)}, u32[]{:S(2)}) collective-permute-start(bf16[1,96,2048]{2,1,0:T(8,128)(2,1)S(1)} %get-tuple-element.6), channel_id=1, source_target_pairs={{0,28},{2,30},{4,24},{6,26},{8,20},{10,22},{12,16},{14,18},{16,12}... | collective-permute-start | bytes 1179656 | tf_op jit(solution)/shard_map/ppermute | solution.py:25
  610.9 50.7 %collective-permute-start.14 = (bf16[1,96,2048]{2,1,0:T(8,128)(2,1)S(1)}, bf16[1,96,2048]{2,1,0:T(8,128)(2,1)S(1)}, u32[]{:S(2)}, u32[]{:S(2)}) collective-permute-start(bf16[1,96,2048]{2,1,0:T(8,128)(2,1)S(1)} %get-tuple-element.5), channel_id=1, source_target_pairs={{0,30},{2,28},{4,26},{6,24},{8,22},{10,20},{12,18},{14,16},{16,14}... | collective-permute-start | bytes 1179656 | tf_op jit(solution)/shard_map/ppermute | solution.py:25
  668.7 17.0 %copy-start.1 = (bf16[128,4096]{1,0:T(8,128)(2,1)S(1)}, bf16[128,4096]{1,0:T(8,128)(2,1)}, u32[]{:S(2)}) copy-start(bf16[128,4096]{1,0:T(8,128)(2,1)} %param.6) | copy-start | bytes 3145732
Sparse Core Ops, SparseCore 0:
  354.4 145.0 reduce-scatter.1
